TPU v7x, 512 devices: a whole 4x8x8 slice. The times are simulated.
512 devices in a mesh: section: 8 (over x, core), expert: 64 (over z, y).
Axes of the slice: x: 4, y: 8, z: 8, core: 2. Of those that a mesh axis runs over, the one named last changes fastest.
Arguments:
- histories: bfloat16 [8, 8192, 5120], P('section', 'expert'), may hold values from -6 to 6
- page_map: int32 [8, 2, 2048], P('section', None, 'expert'), may hold values from 0 to 2047, as said below
- user_pages: int32 [8, 64, 4], P('section', 'expert'), may hold values from 1 to 16, 32 in all within a row
- tails: int32 [8, 64, 4], P('section', 'expert'), may hold values from 1 to 4
- routes: int32 [8, 8192, 2], P('section', 'expert'), may hold values from 0 to 31, all different within a row; in each aligned block of 128 rows (0 to 127, 128 to 255, ..., all dimensions but the last counted through in order) at most 16 rows name the same one
- out_proj: bfloat16 [8, 1024, 1024], P('section', 'expert'), may hold values from -0.1875 to 0.1875
- router: bfloat16 [8, 1024, 32], P('section'), may hold values from -0.75 to 0.75
- w_gate: bfloat16 [8, 1024, 32768], P('section', None, 'expert'), may hold values from -0.1875 to 0.1875
- w_up: bfloat16 [8, 1024, 32768], P('section', None, 'expert'), may hold values from -0.1875 to 0.1875
- w_down: bfloat16 [8, 32768, 1024], P('section', 'expert'), may hold values from -0.1875 to 0.1875
Outputs:
- handed: bfloat16 [8, 8192, 1024], P('section', 'expert')
Inputs may be any that keep to these rules, and one draw needn't show every extreme that they name: page_map[0] is a permutation of the pages of a section and page_map[1] its inverse; every device holds exactly 32 pages before and after; no device's pages send more than 1 pages to one device, and some send exactly 1. `user_pages`: the 4 entries of one device sum to 32, and the largest is 16. `routes`: A row names 2 different experts; among the rows of one device, no expert is named more than 16 times, a bound that some block reaches.
All inputs are finite; a program needn't handle non-finite values.
Results may differ from a plain program's by a relative error of at most 0.012.
Values may be sent and summed in bfloat16 or wider, within the bound.
No kernel may reach another device: no remote copies, remote signals or barrier semaphores. Data moves between devices by JAX's collectives and lax.ppermute only.
A program may use at most 64 MiB of HBM per device.

v0:
```python
import jax
import jax.numpy as jnp
from jax import lax
from jax.sharding import PartitionSpec as P

HEADS = 8


def swapped(shard, axis, apart):
    return lax.ppermute(shard, axis, [(i, i ^ 1 << apart) for i in range(lax.axis_size(axis))])


def from_behind(block, axis, distance):
    devices = range(lax.axis_size(axis))
    route = [((i - distance) % len(devices), i) for i in devices]
    return lax.ppermute(block, axis, route)


def layout_rows(counts, tail_rows, page_rows, row_count):
    starting = jnp.cumsum(counts) - counts
    length = (counts - 1) * page_rows + tail_rows
    row_index = jnp.arange(row_count, dtype=jnp.int32)
    page_of = row_index // page_rows
    owner_of = jnp.sum((starting[None, :] <= page_of[:, None]).astype(jnp.int32), axis=1) - 1
    member = owner_of[:, None] == jnp.arange(counts.shape[0], dtype=jnp.int32)[None, :]
    offset = jnp.sum(jnp.where(member, starting[None, :] * page_rows, 0), axis=1)
    spread = jnp.sum(jnp.where(member, length[None, :], 0), axis=1)
    return (owner_of, row_index - offset, spread)


def attend(balanced, counts, tail_rows, page_rows):
    row_count = balanced.shape[0]
    model_width = balanced.shape[1] // 5
    head_dim = model_width // HEADS
    owner_of, position, spread = layout_rows(counts, tail_rows, page_rows, row_count)
    allowed = (
        (owner_of[:, None] == owner_of[None, :])
        & (position[None, :] <= position[:, None])
        & (position[None, :] < spread[None, :])
    )
    queries = balanced[:, :model_width].reshape(row_count, HEADS, head_dim)
    key_rows = balanced[:, model_width : 2 * model_width].reshape(row_count, HEADS, head_dim)
    values = balanced[:, 2 * model_width : 3 * model_width].reshape(row_count, HEADS, head_dim)
    scores = jnp.einsum(
        "qhd,khd->hqk", queries, key_rows, preferred_element_type=jnp.float32
    ) * head_dim ** (-0.5)
    weights = (
        jnp.where(allowed[None], jax.nn.silu(scores), 0.0)
        / spread.astype(jnp.float32)[None, :, None]
    )
    weights = weights.astype(jnp.bfloat16)
    attended = jnp.einsum(
        "hqk,khd->qhd", weights, values, preferred_element_type=jnp.float32
    ).reshape(row_count, model_width)
    average = jnp.mean(attended, axis=1, keepdims=True)
    centered = attended - average
    variance = jnp.mean(centered * centered, axis=1, keepdims=True)
    gating = balanced[:, 3 * model_width : 4 * model_width].astype(jnp.float32)
    return (centered * lax.rsqrt(variance + 1e-05) * gating).astype(jnp.bfloat16)


def gate_share(normed, router, routes):
    logits = jnp.dot(normed, router, preferred_element_type=jnp.float32)
    scores = jax.nn.sigmoid(logits)
    picked = routes[:, :, None] == jnp.arange(router.shape[1], dtype=jnp.int32)[None, None, :]
    chosen = jnp.sum(jnp.where(picked, scores[:, None, :], 0.0), axis=2)
    return chosen / jnp.sum(chosen, axis=1, keepdims=True)


def slot_table(routes, experts, capacity):
    pair_count = routes.shape[0] * routes.shape[1]
    chosen = routes.reshape(-1)
    onehot = (chosen[:, None] == jnp.arange(experts, dtype=jnp.int32)[None, :]).astype(jnp.int32)
    before = jnp.cumsum(onehot, axis=0) - onehot
    ranking = jnp.sum(before * onehot, axis=1)
    slot_of_pair = chosen * capacity + ranking
    matches = slot_of_pair[None, :] == jnp.arange(experts * capacity, dtype=jnp.int32)[:, None]
    source_token = (
        jnp.sum(jnp.where(matches, jnp.arange(pair_count, dtype=jnp.int32)[None, :], 0), axis=1)
        // 2
    )
    return (slot_of_pair, source_token)


def whole_expert(incoming, gate_full, up_full, down_full):
    flat_rows = incoming.reshape(-1, incoming.shape[-1])
    gate_act = jnp.dot(flat_rows, gate_full, preferred_element_type=jnp.float32)
    up_act = jnp.dot(flat_rows, up_full, preferred_element_type=jnp.float32)
    hidden = (jax.nn.silu(gate_act) * up_act).astype(jnp.bfloat16)
    half_units = gate_full.shape[1] // 2
    first_part = jnp.dot(
        hidden[:, :half_units], down_full[:half_units], preferred_element_type=jnp.float32
    ).astype(jnp.bfloat16)
    second_part = jnp.dot(
        hidden[:, half_units:], down_full[half_units:], preferred_element_type=jnp.float32
    ).astype(jnp.bfloat16)
    summed = (first_part.astype(jnp.float32) + second_part.astype(jnp.float32)).astype(jnp.bfloat16)
    return summed.reshape(incoming.shape)


def shards(histories, page_map, user_pages, tails, routes, out_proj, router, w_gate, w_up, w_down):
    devices = lax.axis_size("expert")
    parity = lax.axis_index("expert") % 2
    row_count = histories.shape[1]
    stacked_width = histories.shape[2]
    model_width = stacked_width // 5
    pages_dev = page_map.shape[2]
    page_rows = row_count // pages_dev
    page_slots = (pages_dev + devices - 1) // devices
    page_block = histories[0].reshape(pages_dev, page_rows, stacked_width)
    target = page_map[0, 0]
    target_dev = target // pages_dev
    earlier = (target_dev[None, :] == target_dev[:, None]) & (target[None, :] < target[:, None])
    position = target_dev * page_slots + jnp.sum(earlier.astype(jnp.int32), axis=1)
    matches = position[None, :] == jnp.arange(devices * page_slots, dtype=jnp.int32)[:, None]
    chosen_page = jnp.sum(
        jnp.where(matches, jnp.arange(pages_dev, dtype=jnp.int32)[None, :], 0), axis=1
    )
    outgoing = page_block[chosen_page]
    arrived = lax.all_to_all(outgoing, "expert", split_axis=0, concat_axis=0, tiled=True)
    anchor = page_map[0, 1]
    anchor_dev = anchor // pages_dev
    ordering = jnp.arange(pages_dev, dtype=jnp.int32)
    sooner = (anchor_dev[None, :] == anchor_dev[:, None]) & (ordering[None, :] < ordering[:, None])
    where_from = anchor_dev * page_slots + jnp.sum(sooner.astype(jnp.int32), axis=1)
    balanced = arrived[where_from].reshape(row_count, stacked_width)
    mixed_in = attend(balanced, user_pages[0, 0], tails[0, 0], page_rows)
    projected = jnp.dot(
        mixed_in,
        lax.all_gather(out_proj, "expert", axis=1, tiled=True)[0],
        preferred_element_type=jnp.float32,
    )
    resid = (balanced[:, 4 * model_width :].astype(jnp.float32) + projected).astype(jnp.bfloat16)
    resid_wide = resid.astype(jnp.float32)
    normed = (
        resid_wide * lax.rsqrt(jnp.mean(resid_wide * resid_wide, axis=1, keepdims=True) + 1e-06)
    ).astype(jnp.bfloat16)
    experts = router.shape[2]
    capacity = 4 * row_count // experts
    share = gate_share(normed, router[0], routes[0])
    slot_of_pair, source_token = slot_table(routes[0], experts, capacity)
    packed = normed[source_token].reshape(experts, capacity, model_width)
    is_odd = parity == 1
    half_units = w_gate.shape[2]
    gate_up = jnp.concatenate([w_gate[0], w_up[0]], axis=1)
    other_gate_up = swapped(gate_up, "expert", 0)
    other_down = swapped(w_down[0], "expert", 0)
    own_gate = gate_up[:, :half_units]
    own_up = gate_up[:, half_units:]
    other_gate = other_gate_up[:, :half_units]
    other_up = other_gate_up[:, half_units:]
    gate_full = jnp.where(
        is_odd,
        jnp.concatenate([other_gate, own_gate], axis=1),
        jnp.concatenate([own_gate, other_gate], axis=1),
    )
    up_full = jnp.where(
        is_odd,
        jnp.concatenate([other_up, own_up], axis=1),
        jnp.concatenate([own_up, other_up], axis=1),
    )
    down_full = jnp.where(
        is_odd,
        jnp.concatenate([other_down, w_down[0]], axis=0),
        jnp.concatenate([w_down[0], other_down], axis=0),
    )
    half_cap = capacity // 2
    sent_rows = packed.reshape(experts * 2, half_cap, model_width)
    own_rows = lax.all_to_all(sent_rows, "expert", split_axis=0, concat_axis=0, tiled=True)
    served = whole_expert(own_rows, gate_full, up_full, down_full)
    came_back = lax.all_to_all(served, "expert", split_axis=0, concat_axis=0, tiled=True)
    result = came_back.reshape(experts, capacity, model_width)
    picked = result.reshape(experts * capacity, model_width)[slot_of_pair]
    picked = picked.reshape(row_count, 2, model_width).astype(jnp.float32)
    mixture = jnp.sum(picked * share[:, :, None], axis=1)
    output_rows = (resid_wide + mixture).astype(jnp.bfloat16)
    return from_behind(output_rows[None], "section", 1)


def solution(mesh):
    in_specs = (
        P("section", "expert", None),
        P("section", None, "expert"),
        P("section", "expert", None),
        P("section", "expert", None),
        P("section", "expert", None),
        P("section", "expert", None),
        P("section", None, None),
        P("section", None, "expert"),
        P("section", None, "expert"),
        P("section", "expert", None),
    )
    out_specs = P("section", "expert", None)
    return jax.shard_map(shards, mesh=mesh, in_specs=in_specs, out_specs=out_specs, check_vma=False)
```

profile of v0, /device:TPU:8, one launch (start us, length us, event | category | flops | bytes accessed | tf_op | source)
XLA Modules:
  0.0 289.1 jit_solution(12892616485323434839)
XLA Ops:
  6.5 0.8 and_select_fusion.2
  7.3 0.7 slice_bitcast_fusion
  8.3 2.6 reshape_squeeze.6
  10.9 4.2 %gather_fusion = bf16[64,4,5120]{2,1,0:T(4,128)(2,1)} fusion(bf16[32,4,5120]{2,1,0:T(4,128)(2,1)S(1)} %reshape_squeeze.6, s32[1024]{0:T(1024)S(1)} %pad_clamp_fusion.3), kind=kCustom, calls=%fused_computation | custom fusion | bytes 5243136 | tf_op jit(solution)/shard_map/gather | solution.py:119
  15.1 16.6 %all-to-all-start = ((bf16[64,4,5120]{2,1,0:T(4,128)(2,1)}), bf16[64,4,5120]{2,1,0:T(4,128)(2,1)S(1)}, u32[]{:S(2)}, u32[]{:S(2)}) async-start(bf16[64,4,5120]{2,1,0:T(4,128)(2,1)} %gather_fusion), calls=%async_computation | async-start | bytes 5242880 | tf_op jit(solution)/shard_map/all_to_all | solution.py:120
  31.7 0.7 all-gather.2.cloned.1.call-update
  32.5 3.1 %pad_maximum_fusion.1 = bf16[1024,1024]{1,0:T(8,128)(2,1)} fusion(bf16[1024,512]{1,0:T(8,128)(2,1)} %bitcast.121, bf16[1024,512]{1,0:T(8,128)(2,1)} %bitcast.119), kind=kLoop, calls=%fused_computation.5 | loop fusion | flops 4194304 | bytes 4194304 | tf_op jit(solution)/shard_map/concatenate | solution.py:145
  35.6 2.4 collective-permute-start
  38.7 0.6 reduce-window.18
  40.0 57.6 %all-to-all-done = bf16[64,4,5120]{2,1,0:T(4,128)(2,1)S(1)} async-done(((bf16[64,4,5120]{2,1,0:T(4,128)(2,1)}), bf16[64,4,5120]{2,1,0:T(4,128)(2,1)S(1)}, u32[]{:S(2)}, u32[]{:S(2)}) %all-to-all-start) | async-done | bytes 2621472 | tf_op jit(solution)/shard_map/all_to_all | solution.py:120
  97.6 2.7 gather_fusion.1
  100.3 2.5 reshape.543
  103.4 0.6 fusion.70
  104.4 52.7 %all-gather.2.cloned.1.call-done = bf16[1,1024,1024]{2,1,0:T(8,128)(2,1)} async-done(((bf16[1,16,1024]{2,1,0:T(8,128)(2,1)}), bf16[1,1024,1024]{2,1,0:T(8,128)(2,1)}) %all-gather.2.cloned.1.call-update) | async-done | bytes 2097168 | tf_op jit(solution)/shard_map/all_gather | solution.py:130
  157.1 2.2 multiply_reduce_fusion.1
  159.4 2.8 gather_fusion.2
  162.2 10.1 %all-to-all-start.1 = ((bf16[64,8,1024]{2,1,0:T(8,128)(2,1)}), bf16[64,8,1024]{2,1,0:T(8,128)(2,1)}, u32[]{:S(2)}, u32[]{:S(2)}) async-start(bf16[64,8,1024]{2,1,0:T(8,128)(2,1)} %bitcast.20), calls=%async_computation.1 | async-start | bytes 2097152 | tf_op jit(solution)/shard_map/all_to_all | solution.py:169
  172.2 2.6 collective-permute-start.1
  174.9 39.3 %collective-permute-done.1 = bf16[512,1024]{1,0:T(8,128)(2,1)} collective-permute-done((bf16[512,1024]{1,0:T(8,128)(2,1)S(1)}, bf16[512,1024]{1,0:T(8,128)(2,1)}, u32[]{:S(2)}, u32[]{:S(2)}) %collective-permute-start.1) | collective-permute-done | bytes 1048608 | tf_op jit(solution)/shard_map/ppermute | solution.py:10
  214.2 4.1 %maximum_select_fusion = bf16[1024,1024]{1,0:T(8,128)(2,1)} fusion(bf16[512,1024]{1,0:T(8,128)(2,1)S(1)} %bitcast.118, bf16[512,1024]{1,0:T(8,128)(2,1)} %collective-permute-done.1, pred[]{:T(512)S(6)} %eq.150), kind=kLoop, calls=%fused_computation.19 | loop fusion | flops 9437184 | bytes 4194305 | tf_op jit(solution)/shard_map/jit(_where)/select_n | solution.py:162
  218.3 3.1 %fusion.68 = (bf16[1024,512]{1,0:T(8,128)(2,1)}, bf16[1024,512]{1,0:T(8,128)(2,1)}) fusion(bf16[1024,1024]{1,0:T(8,128)(2,1)} %collective-permute-done), kind=kLoop, calls=%fused_computation.141 | loop fusion | bytes 4194304 | tf_op jit(solution)/shard_map/slice | solution.py:151
  221.3 3.3 %fusion.1 = f32[512,1024]{1,0:T(8,128)S(1)} fusion(bf16[1024,512]{1,0:T(8,128)(2,1)S(1)} %bitcast.120, bf16[1024,512]{1,0:T(8,128)(2,1)} %get-tuple-element.12, pred[]{:T(512)S(6)} %eq.150, bf16[64,8,1024]{2,1,0:T(8,128)(2,1)} %all-to-all-done.1), kind=kOutput, calls=%fused_computation.8 | convolution fusion | flops 1083179008 | bytes 5242881 | tf_op jit(solution)/shard_map/dot_general | solution.py:87
  224.7 3.8 %multiply_convert_fusion = bf16[512,1024]{1,0:T(8,128)(2,1)S(1)} fusion(f32[512,1024]{1,0:T(8,128)S(1)} %fusion.1, bf16[1024,512]{1,0:T(8,128)(2,1)S(1)} %bitcast.122, bf16[1024,512]{1,0:T(8,128)(2,1)S(1)} %copy-done.5, pred[]{:T(512)S(6)} %eq.150, bf16[64,8,1024]{2,1,0:T(8,128)(2,1)} %all-to-all-done.1), kind=kOutput, calls=%fused_computation.23 | convolution fusion | flops 1086324736 | bytes 6291457 | tf_op jit(solution)/shard_map/dot_general | solution.py:88
  228.4 0.7 convolution_convert_fusion.1
  229.2 1.7 fusion.18
  230.9 12.6 %all-to-all-start.2 = ((bf16[64,8,1024]{2,1,0:T(8,128)(2,1)}), bf16[64,8,1024]{2,1,0:T(8,128)(2,1)S(1)}, u32[]{:S(2)}, u32[]{:S(2)}) async-start(bf16[64,8,1024]{2,1,0:T(8,128)(2,1)} %fusion.18), calls=%async_computation.2 | async-start | bytes 2097152 | tf_op jit(solution)/shard_map/all_to_all | solution.py:171
  244.2 27.0 %all-to-all-done.2 = bf16[64,8,1024]{2,1,0:T(8,128)(2,1)S(1)} async-done(((bf16[64,8,1024]{2,1,0:T(8,128)(2,1)}), bf16[64,8,1024]{2,1,0:T(8,128)(2,1)S(1)}, u32[]{:S(2)}, u32[]{:S(2)}) %all-to-all-start.2) | async-done | bytes 1048608 | tf_op jit(solution)/shard_map/all_to_all | solution.py:171
  271.3 1.2 gather_fusion.3
  272.4 0.7 reshape.553
  273.1 1.3 multiply_reduce_fusion
  274.5 7.0 %collective-permute-done.2 = bf16[1,128,1024]{2,1,0:T(8,128)(2,1)S(1)} collective-permute-done((bf16[1,128,1024]{2,1,0:T(8,128)(2,1)S(1)}, bf16[1,128,1024]{2,1,0:T(8,128)(2,1)S(1)}, u32[]{:S(2)}, u32[]{:S(2)}) %collective-permute-start.2) | collective-permute-done | bytes 262176 | tf_op jit(solution)/shard_map/ppermute | solution.py:16
  281.5 0.7 copy.43
  (73 shorter events, 3.5 us)
Async XLA Ops:
  6.5 237.3 %copy-start = (bf16[1,1024,32]{1,2,0:T(8,128)(2,1)S(1)}, bf16[1,1024,32]{1,2,0:T(8,128)(2,1)}, u32[]{:S(2)}) copy-start(bf16[1,1024,32]{1,2,0:T(8,128)(2,1)} %param.16) | copy-start | bytes 196612
  15.1 82.5 %all-to-all-start = ((bf16[64,4,5120]{2,1,0:T(4,128)(2,1)}), bf16[64,4,5120]{2,1,0:T(4,128)(2,1)S(1)}, u32[]{:S(2)}, u32[]{:S(2)}) async-start(bf16[64,4,5120]{2,1,0:T(4,128)(2,1)} %gather_fusion), calls=%async_computation | async-start | bytes 5242880 | tf_op jit(solution)/shard_map/all_to_all | solution.py:120
  31.7 125.4 %all-gather.2.cloned.1.call-start = ((), (), s32[]{:S(2)}) async-start(), calls=%async_computation.3 | async-start | bytes 2129920 | tf_op jit(solution)/shard_map/all_gather | solution.py:130
  32.4 5.5 %copy-start.6 = (s32[1,128,2]{1,2,0:T(2,128)S(1)}, s32[1,128,2]{1,2,0:T(2,128)}, u32[]{:S(2)}) copy-start(s32[1,128,2]{1,2,0:T(2,128)} %param.14) | copy-start | bytes 3076
  32.4 5.9 %copy-start.8 = (s32[1,1,4]{2,1,0:T(1,128)S(1)}, s32[1,1,4]{2,1,0:T(1,128)}, u32[]{:S(2)}) copy-start(s32[1,1,4]{2,1,0:T(1,128)} %param.12) | copy-start | bytes 52
  32.4 6.1 %copy-start.9 = (s32[1,1,4]{2,1,0:T(1,128)S(1)}, s32[1,1,4]{2,1,0:T(1,128)}, u32[]{:S(2)}) copy-start(s32[1,1,4]{2,1,0:T(1,128)} %param.13) | copy-start | bytes 52
  32.5 7.1 %copy-start.7 = (s32[1,2,32]{2,1,0:T(2,128)S(1)}, s32[1,2,32]{2,1,0:T(2,128)}, u32[]{:S(2)}) copy-start(s32[1,2,32]{2,1,0:T(2,128)} %param.11) | copy-start | bytes 772
  35.6 182.7 %collective-permute-start = (bf16[1024,1024]{1,0:T(8,128)(2,1)}, bf16[1024,1024]{1,0:T(8,128)(2,1)}, u32[]{:S(2)}, u32[]{:S(2)}) collective-permute-start(bf16[1024,1024]{1,0:T(8,128)(2,1)} %pad_maximum_fusion.1), channel_id=1, source_target_pairs={{0,1},{1,0},{2,3},{3,2},{4,5},{5,4},{6,7},{7,6},{8,9},{9,8},{10,11... | collective-permute-start | bytes 6291464 | tf_op jit(solution)/shard_map/ppermute | solution.py:10
  162.2 10.1 %copy-start.2 = (bf16[1,512,1024]{2,1,0:T(8,128)(2,1)S(1)}, bf16[1,512,1024]{2,1,0:T(8,128)(2,1)}, u32[]{:S(2)}) copy-start(bf16[1,512,1024]{2,1,0:T(8,128)(2,1)} %param.19) | copy-start | bytes 3145732
  162.2 59.2 %all-to-all-start.1 = ((bf16[64,8,1024]{2,1,0:T(8,128)(2,1)}), bf16[64,8,1024]{2,1,0:T(8,128)(2,1)}, u32[]{:S(2)}, u32[]{:S(2)}) async-start(bf16[64,8,1024]{2,1,0:T(8,128)(2,1)} %bitcast.20), calls=%async_computation.1 | async-start | bytes 2097152 | tf_op jit(solution)/shard_map/all_to_all | solution.py:169
  172.2 41.9 %collective-permute-start.1 = (bf16[512,1024]{1,0:T(8,128)(2,1)S(1)}, bf16[512,1024]{1,0:T(8,128)(2,1)}, u32[]{:S(2)}, u32[]{:S(2)}) collective-permute-start(bf16[512,1024]{1,0:T(8,128)(2,1)S(1)} %bitcast.117), channel_id=1, source_target_pairs={{0,1},{1,0},{2,3},{3,2},{4,5},{5,4},{6,7},{7,6},{8,9},{9,8},{10,11... | collective-permute-start | bytes 3145736 | tf_op jit(solution)/shard_map/ppermute | solution.py:10
  218.3 3.1 %copy-start.3 = (bf16[1,1024,512]{2,1,0:T(8,128)(2,1)S(1)}, bf16[1,1024,512]{2,1,0:T(8,128)(2,1)}, u32[]{:S(2)}) copy-start(bf16[1,1024,512]{2,1,0:T(8,128)(2,1)} %param.17) | copy-start | bytes 3145732
  221.3 3.3 %copy-start.4 = (bf16[1,1024,512]{2,1,0:T(8,128)(2,1)S(1)}, bf16[1,1024,512]{2,1,0:T(8,128)(2,1)}, u32[]{:S(2)}) copy-start(bf16[1,1024,512]{2,1,0:T(8,128)(2,1)} %param.18) | copy-start | bytes 3145732
  221.3 3.3 %copy-start.5 = (bf16[1024,512]{1,0:T(8,128)(2,1)S(1)}, bf16[1024,512]{1,0:T(8,128)(2,1)}, u32[]{:S(2)}) copy-start(bf16[1024,512]{1,0:T(8,128)(2,1)} %get-tuple-element.11) | copy-start | bytes 3145732
  224.7 3.8 %copy-start.1 = (bf16[1024,1024]{1,0:T(8,128)(2,1)S(1)}, bf16[1024,1024]{1,0:T(8,128)(2,1)}, u32[]{:S(2)}) copy-start(bf16[1024,1024]{1,0:T(8,128)(2,1)} %maximum_select_fusion) | copy-start | bytes 6291460
  230.9 40.4 %all-to-all-start.2 = ((bf16[64,8,1024]{2,1,0:T(8,128)(2,1)}), bf16[64,8,1024]{2,1,0:T(8,128)(2,1)S(1)}, u32[]{:S(2)}, u32[]{:S(2)}) async-start(bf16[64,8,1024]{2,1,0:T(8,128)(2,1)} %fusion.18), calls=%async_computation.2 | async-start | bytes 2097152 | tf_op jit(solution)/shard_map/all_to_all | solution.py:171
  274.5 7.0 %collective-permute-start.2 = (bf16[1,128,1024]{2,1,0:T(8,128)(2,1)S(1)}, bf16[1,128,1024]{2,1,0:T(8,128)(2,1)S(1)}, u32[]{:S(2)}, u32[]{:S(2)}) collective-permute-start(bf16[1,128,1024]{2,1,0:T(8,128)(2,1)S(1)} %fusion.44), channel_id=1, source_target_pairs={{448,0},{0,64},{64,128},{128,192},{192,256},{256,320},{320,384},{3... | collective-permute-start | bytes 786440 | tf_op jit(solution)/shard_map/ppermute | solution.py:16
Sparse Core Ops, SparseCore 0:
  35.6 121.4 all-gather.1
where the time goes:
time: 290 us; the launch traced here: 289 us
  waiting for transfers between devices  184 us (63%)
  starting transfers between devices  44.3 us (15%)
  local copies, waits for them, and re-layouts  22.7 us (8%)
  between operations  13.8 us (5%)
  matrix products  12.5 us (4%)
  other arithmetic  11.4 us (4%)
    all_to_all x1, waiting for transfers between devices, shards(): lax.all_to_all(outgoing, 'expert', split_axis=0, concat_axis=0, tiled=True)  57.6 us
    all_gather x1, waiting for transfers between devices, shards(): lax.all_gather(out_proj, 'expert', axis=1, tiled=True)[0]  52.7 us
    ppermute x2, waiting for transfers between devices, swapped(): lax.ppermute(shard, axis, [(i, i ^ 1 << apart) for i in range(lax.axis_si...  39.3 us
    all_to_all x1, waiting for transfers between devices, shards(): lax.all_to_all(served, 'expert', split_axis=0, concat_axis=0, tiled=True)  27 us
    all_to_all x1, starting transfers between devices, shards(): lax.all_to_all(outgoing, 'expert', split_axis=0, concat_axis=0, tiled=True)  16.6 us
    all_to_all x1, starting transfers between devices, shards(): lax.all_to_all(served, 'expert', split_axis=0, concat_axis=0, tiled=True)  12.6 us
    all_to_all x1, starting transfers between devices, shards(): lax.all_to_all(sent_rows, 'expert', split_axis=0, concat_axis=0, tiled=True)  10.1 us
    ppermute x1, waiting for transfers between devices, from_behind(): return lax.ppermute(block, axis, route)  6.99 us
  transfers between devices with their start and end apart: 7, of which 5 were waited for; matrix products, arithmetic and copies ran while one was open for 9% of the time, Pallas kernels for 0%

commit v1 on v0

--- a/solution.py
+++ b/solution.py
@@ -2,6 +2,7 @@
 import jax.numpy as jnp
 from jax import lax
 from jax.sharding import PartitionSpec as P
+from jax.lax import all_gather
 
 HEADS = 8
 
@@ -127,7 +128,7 @@
     mixed_in = attend(balanced, user_pages[0, 0], tails[0, 0], page_rows)
     projected = jnp.dot(
         mixed_in,
-        lax.all_gather(out_proj, "expert", axis=1, tiled=True)[0],
+        jnp.concatenate(all_gather(out_proj, "expert"), axis=1)[0],
         preferred_element_type=jnp.float32,
     )
     resid = (balanced[:, 4 * model_width :].astype(jnp.float32) + projected).astype(jnp.bfloat16)

time: 290 us -> 289 us (level)
  transfers between devices with their start and end apart: 7 -> 7, of which waited for: 5 -> 5; matrix products, arithmetic and copies ran while one was open for 9% -> 8% of each run, Pallas kernels for 0% -> 0%
where the time goes in v1:
time: 289 us
  waiting for transfers between devices  184 us (64%)
  starting transfers between devices  44.3 us (15%)
  local copies, waits for them, and re-layouts  22.7 us (8%)
  between operations  13.8 us (5%)
  matrix products  13 us (4%)
  other arithmetic  10.7 us (4%)
    all_to_all x1, waiting for transfers between devices, shards(): lax.all_to_all(outgoing, 'expert', split_axis=0, concat_axis=0, tiled=True)  57.5 us
    all_gather x1, waiting for transfers between devices, shards(): all_gather(out_proj, 'expert')  52.7 us
    ppermute x2, waiting for transfers between devices, swapped(): lax.ppermute(shard, axis, [(i, i ^ 1 << apart) for i in range(lax.axis_si...  39.3 us
    all_to_all x1, waiting for transfers between devices, shards(): lax.all_to_all(served, 'expert', split_axis=0, concat_axis=0, tiled=True)  27 us
    all_to_all x1, starting transfers between devices, shards(): lax.all_to_all(outgoing, 'expert', split_axis=0, concat_axis=0, tiled=True)  16.6 us
    all_to_all x1, starting transfers between devices, shards(): lax.all_to_all(served, 'expert', split_axis=0, concat_axis=0, tiled=True)  12.6 us
    all_to_all x1, starting transfers between devices, shards(): lax.all_to_all(sent_rows, 'expert', split_axis=0, concat_axis=0, tiled=True)  10.1 us
    ppermute x1, waiting for transfers between devices, from_behind(): return lax.ppermute(block, axis, route)  6.99 us
  transfers between devices with their start and end apart: 7, of which 5 were waited for; matrix products, arithmetic and copies ran while one was open for 8% of the time, Pallas kernels for 0%

profile of v1, /device:TPU:8, one launch (start us, length us, event | category | flops | bytes accessed | tf_op | source)
XLA Modules:
  0.0 288.7 jit_solution(14095413754244489750)
XLA Ops:
  6.5 0.8 and_select_fusion.2
  7.3 0.7 slice_bitcast_fusion
  8.3 2.6 reshape_squeeze.6
  10.9 4.2 %gather_fusion = bf16[64,4,5120]{2,1,0:T(4,128)(2,1)} fusion(bf16[32,4,5120]{2,1,0:T(4,128)(2,1)S(1)} %reshape_squeeze.6, s32[1024]{0:T(1024)S(1)} %pad_clamp_fusion.3), kind=kCustom, calls=%fused_computation | custom fusion | bytes 5243136 | tf_op jit(solution)/shard_map/gather | solution.py:120
  15.0 16.6 %all-to-all-start = ((bf16[64,4,5120]{2,1,0:T(4,128)(2,1)}), bf16[64,4,5120]{2,1,0:T(4,128)(2,1)S(1)}, u32[]{:S(2)}, u32[]{:S(2)}) async-start(bf16[64,4,5120]{2,1,0:T(4,128)(2,1)} %gather_fusion), calls=%async_computation | async-start | bytes 5242880 | tf_op jit(solution)/shard_map/all_to_all | solution.py:121
  31.7 0.7 all-gather.3.cloned.1.call-update
  32.4 3.2 %pad_maximum_fusion.1 = bf16[1024,1024]{1,0:T(8,128)(2,1)} fusion(bf16[1024,512]{1,0:T(8,128)(2,1)} %bitcast.113, bf16[1024,512]{1,0:T(8,128)(2,1)} %bitcast.111), kind=kLoop, calls=%fused_computation.5 | loop fusion | flops 4194304 | bytes 4194304 | tf_op jit(solution)/shard_map/concatenate | solution.py:146
  35.6 2.4 collective-permute-start
  38.8 0.6 reduce-window.18
  40.1 57.5 %all-to-all-done = bf16[64,4,5120]{2,1,0:T(4,128)(2,1)S(1)} async-done(((bf16[64,4,5120]{2,1,0:T(4,128)(2,1)}), bf16[64,4,5120]{2,1,0:T(4,128)(2,1)S(1)}, u32[]{:S(2)}, u32[]{:S(2)}) %all-to-all-start) | async-done | bytes 2621472 | tf_op jit(solution)/shard_map/all_to_all | solution.py:121
  97.6 2.7 gather_fusion.1
  100.2 2.5 reshape.543
  103.3 0.6 fusion.61
  104.3 52.7 %all-gather.3.cloned.1.call-done = bf16[64,16,1024]{2,1,0:T(8,128)(2,1)} async-done(((bf16[1,16,1024]{2,1,0:T(8,128)(2,1)}), bf16[64,16,1024]{2,1,0:T(8,128)(2,1)}) %all-gather.3.cloned.1.call-update) | async-done | bytes 2097168 | tf_op jit(solution)/shard_map/all_gather | solution.py:131
  157.0 2.2 multiply_reduce_fusion.1
  159.3 2.8 gather_fusion.2
  162.1 10.1 %all-to-all-start.1 = ((bf16[64,8,1024]{2,1,0:T(8,128)(2,1)}), bf16[64,8,1024]{2,1,0:T(8,128)(2,1)}, u32[]{:S(2)}, u32[]{:S(2)}) async-start(bf16[64,8,1024]{2,1,0:T(8,128)(2,1)} %bitcast.20), calls=%async_computation.1 | async-start | bytes 2097152 | tf_op jit(solution)/shard_map/all_to_all | solution.py:170
  172.2 2.6 collective-permute-start.1
  174.8 39.3 %collective-permute-done.1 = bf16[512,1024]{1,0:T(8,128)(2,1)} collective-permute-done((bf16[512,1024]{1,0:T(8,128)(2,1)S(1)}, bf16[512,1024]{1,0:T(8,128)(2,1)}, u32[]{:S(2)}, u32[]{:S(2)}) %collective-permute-start.1) | collective-permute-done | bytes 1048608 | tf_op jit(solution)/shard_map/ppermute | solution.py:11
  214.1 3.3 %maximum_select_fusion = bf16[1024,1024]{1,0:T(8,128)(2,1)S(1)} fusion(bf16[512,1024]{1,0:T(8,128)(2,1)} %bitcast.109, bf16[512,1024]{1,0:T(8,128)(2,1)} %collective-permute-done.1, pred[]{:T(512)S(6)} %eq.150), kind=kLoop, calls=%fused_computation.19 | loop fusion | flops 9437184 | bytes 4194305 | tf_op jit(solution)/shard_map/jit(_where)/select_n | solution.py:163
  217.4 3.1 %fusion.59 = (bf16[1024,512]{1,0:T(8,128)(2,1)}, bf16[1024,512]{1,0:T(8,128)(2,1)}) fusion(bf16[1024,1024]{1,0:T(8,128)(2,1)} %collective-permute-done), kind=kLoop, calls=%fused_computation.139 | loop fusion | bytes 4194304 | tf_op jit(solution)/shard_map/slice | solution.py:152
  220.5 3.9 %fusion.1 = f32[512,1024]{1,0:T(8,128)S(1)} fusion(bf16[1024,512]{1,0:T(8,128)(2,1)} %bitcast.112, bf16[1024,512]{1,0:T(8,128)(2,1)} %get-tuple-element.12, pred[]{:T(512)S(6)} %eq.150, bf16[64,8,1024]{2,1,0:T(8,128)(2,1)} %all-to-all-done.1), kind=kOutput, calls=%fused_computation.8 | convolution fusion | flops 1083179008 | bytes 5242881 | tf_op jit(solution)/shard_map/dot_general | solution.py:88
  224.4 3.6 %multiply_convert_fusion = bf16[512,1024]{1,0:T(8,128)(2,1)S(1)} fusion(f32[512,1024]{1,0:T(8,128)S(1)} %fusion.1, bf16[1024,512]{1,0:T(8,128)(2,1)S(1)} %bitcast.114, bf16[1024,512]{1,0:T(8,128)(2,1)S(1)} %copy-done.3, pred[]{:T(512)S(6)} %eq.150, bf16[64,8,1024]{2,1,0:T(8,128)(2,1)} %all-to-all-done.1), kind=kOutput, calls=%fused_computation.21 | convolution fusion | flops 1086324736 | bytes 6291457 | tf_op jit(solution)/shard_map/dot_general | solution.py:89
  228.0 0.7 convolution_convert_fusion.1
  228.8 1.7 fusion.16
  230.5 12.6 %all-to-all-start.2 = ((bf16[64,8,1024]{2,1,0:T(8,128)(2,1)}), bf16[64,8,1024]{2,1,0:T(8,128)(2,1)S(1)}, u32[]{:S(2)}, u32[]{:S(2)}) async-start(bf16[64,8,1024]{2,1,0:T(8,128)(2,1)} %fusion.16), calls=%async_computation.2 | async-start | bytes 2097152 | tf_op jit(solution)/shard_map/all_to_all | solution.py:172
  243.8 27.0 %all-to-all-done.2 = bf16[64,8,1024]{2,1,0:T(8,128)(2,1)S(1)} async-done(((bf16[64,8,1024]{2,1,0:T(8,128)(2,1)}), bf16[64,8,1024]{2,1,0:T(8,128)(2,1)S(1)}, u32[]{:S(2)}, u32[]{:S(2)}) %all-to-all-start.2) | async-done | bytes 1048608 | tf_op jit(solution)/shard_map/all_to_all | solution.py:172
  270.8 1.2 gather_fusion.3
  272.0 0.7 reshape.553
  272.7 1.3 multiply_reduce_fusion
  274.1 7.0 %collective-permute-done.2 = bf16[1,128,1024]{2,1,0:T(8,128)(2,1)S(1)} collective-permute-done((bf16[1,128,1024]{2,1,0:T(8,128)(2,1)S(1)}, bf16[1,128,1024]{2,1,0:T(8,128)(2,1)S(1)}, u32[]{:S(2)}, u32[]{:S(2)}) %collective-permute-start.2) | collective-permute-done | bytes 262176 | tf_op jit(solution)/shard_map/ppermute | solution.py:17
  281.1 0.7 copy.55
  (69 shorter events, 3.5 us)
Async XLA Ops:
  6.5 236.9 %copy-start = (bf16[1,1024,32]{1,2,0:T(8,128)(2,1)S(1)}, bf16[1,1024,32]{1,2,0:T(8,128)(2,1)}, u32[]{:S(2)}) copy-start(bf16[1,1024,32]{1,2,0:T(8,128)(2,1)} %param.16) | copy-start | bytes 196612
  15.0 82.5 %all-to-all-start = ((bf16[64,4,5120]{2,1,0:T(4,128)(2,1)}), bf16[64,4,5120]{2,1,0:T(4,128)(2,1)S(1)}, u32[]{:S(2)}, u32[]{:S(2)}) async-start(bf16[64,4,5120]{2,1,0:T(4,128)(2,1)} %gather_fusion), calls=%async_computation | async-start | bytes 5242880 | tf_op jit(solution)/shard_map/all_to_all | solution.py:121
  31.6 125.4 %all-gather.3.cloned.1.call-start = ((), (), s32[]{:S(2)}) async-start(), calls=%async_computation.3 | async-start | bytes 2129920 | tf_op jit(solution)/shard_map/all_gather | solution.py:131
  32.4 5.6 %copy-start.4 = (s32[1,128,2]{1,2,0:T(2,128)S(1)}, s32[1,128,2]{1,2,0:T(2,128)}, u32[]{:S(2)}) copy-start(s32[1,128,2]{1,2,0:T(2,128)} %param.14) | copy-start | bytes 3076
  32.4 6.0 %copy-start.6 = (s32[1,1,4]{2,1,0:T(1,128)S(1)}, s32[1,1,4]{2,1,0:T(1,128)}, u32[]{:S(2)}) copy-start(s32[1,1,4]{2,1,0:T(1,128)} %param.12) | copy-start | bytes 52
  32.4 6.2 %copy-start.7 = (s32[1,1,4]{2,1,0:T(1,128)S(1)}, s32[1,1,4]{2,1,0:T(1,128)}, u32[]{:S(2)}) copy-start(s32[1,1,4]{2,1,0:T(1,128)} %param.13) | copy-start | bytes 52
  32.4 7.2 %copy-start.5 = (s32[1,2,32]{2,1,0:T(2,128)S(1)}, s32[1,2,32]{2,1,0:T(2,128)}, u32[]{:S(2)}) copy-start(s32[1,2,32]{2,1,0:T(2,128)} %param.11) | copy-start | bytes 772
  35.6 181.8 %collective-permute-start = (bf16[1024,1024]{1,0:T(8,128)(2,1)}, bf16[1024,1024]{1,0:T(8,128)(2,1)}, u32[]{:S(2)}, u32[]{:S(2)}) collective-permute-start(bf16[1024,1024]{1,0:T(8,128)(2,1)} %pad_maximum_fusion.1), channel_id=1, source_target_pairs={{0,1},{1,0},{2,3},{3,2},{4,5},{5,4},{6,7},{7,6},{8,9},{9,8},{10,11... | collective-permute-start | bytes 6291464 | tf_op jit(solution)/shard_map/ppermute | solution.py:11
  162.1 10.1 %copy-start.1 = (bf16[1,512,1024]{2,1,0:T(8,128)(2,1)S(1)}, bf16[1,512,1024]{2,1,0:T(8,128)(2,1)}, u32[]{:S(2)}) copy-start(bf16[1,512,1024]{2,1,0:T(8,128)(2,1)} %param.19) | copy-start | bytes 3145732
  162.1 58.3 %all-to-all-start.1 = ((bf16[64,8,1024]{2,1,0:T(8,128)(2,1)}), bf16[64,8,1024]{2,1,0:T(8,128)(2,1)}, u32[]{:S(2)}, u32[]{:S(2)}) async-start(bf16[64,8,1024]{2,1,0:T(8,128)(2,1)} %bitcast.20), calls=%async_computation.1 | async-start | bytes 2097152 | tf_op jit(solution)/shard_map/all_to_all | solution.py:170
  172.2 41.9 %collective-permute-start.1 = (bf16[512,1024]{1,0:T(8,128)(2,1)S(1)}, bf16[512,1024]{1,0:T(8,128)(2,1)}, u32[]{:S(2)}, u32[]{:S(2)}) collective-permute-start(bf16[512,1024]{1,0:T(8,128)(2,1)S(1)} %bitcast.110), channel_id=1, source_target_pairs={{0,1},{1,0},{2,3},{3,2},{4,5},{5,4},{6,7},{7,6},{8,9},{9,8},{10,11... | collective-permute-start | bytes 3145736 | tf_op jit(solution)/shard_map/ppermute | solution.py:11
  220.5 3.9 %copy-start.2 = (bf16[1,1024,512]{2,1,0:T(8,128)(2,1)S(1)}, bf16[1,1024,512]{2,1,0:T(8,128)(2,1)}, u32[]{:S(2)}) copy-start(bf16[1,1024,512]{2,1,0:T(8,128)(2,1)} %param.18) | copy-start | bytes 3145732
  220.5 3.9 %copy-start.3 = (bf16[1024,512]{1,0:T(8,128)(2,1)S(1)}, bf16[1024,512]{1,0:T(8,128)(2,1)}, u32[]{:S(2)}) copy-start(bf16[1024,512]{1,0:T(8,128)(2,1)} %get-tuple-element.11) | copy-start | bytes 3145732
  230.5 40.4 %all-to-all-start.2 = ((bf16[64,8,1024]{2,1,0:T(8,128)(2,1)}), bf16[64,8,1024]{2,1,0:T(8,128)(2,1)S(1)}, u32[]{:S(2)}, u32[]{:S(2)}) async-start(bf16[64,8,1024]{2,1,0:T(8,128)(2,1)} %fusion.16), calls=%async_computation.2 | async-start | bytes 2097152 | tf_op jit(solution)/shard_map/all_to_all | solution.py:172
  274.1 7.0 %collective-permute-start.2 = (bf16[1,128,1024]{2,1,0:T(8,128)(2,1)S(1)}, bf16[1,128,1024]{2,1,0:T(8,128)(2,1)S(1)}, u32[]{:S(2)}, u32[]{:S(2)}) collective-permute-start(bf16[1,128,1024]{2,1,0:T(8,128)(2,1)S(1)} %fusion.35), channel_id=1, source_target_pairs={{448,0},{0,64},{64,128},{128,192},{192,256},{256,320},{320,384},{3... | collective-permute-start | bytes 786440 | tf_op jit(solution)/shard_map/ppermute | solution.py:17
Sparse Core Ops, SparseCore 0:
  35.5 121.4 all-gather.2
